TPU v7x, 128 devices: a whole 4x4x4 slice. The times are simulated.
128 devices in a mesh: mem: 4 (over y), col: 32 (over z, x, core).
Axes of the slice: x: 4, y: 4, z: 4, core: 2. Of those that a mesh axis runs over, the one named last changes fastest.
Arguments:
- ensemble: bfloat16 [256, 3, 128, 4096], P('mem', None, None, 'col'), may hold values from -6 to 6
- increment: bfloat16 [3, 128, 4096], P(None, 'mem', 'col'), may hold values from -6 to 6
- vert_root: bfloat16 [3, 128, 128], replicated, may hold values from -1 to 2, as said below
- tiles: bfloat16 [32, 8, 128, 128], replicated, may hold values from -2 to 3, as said below
- tile_col: int32 [32, 8], replicated, may hold values from 0 to 31
- level_reach: int32 [128], replicated, may hold values from 2 to 8, as said below
Outputs:
- covaried: bfloat16 [3, 128, 4096], P(None, 'mem', 'col')
Inputs may be any that keep to these rules, and one draw needn't show every extreme that they name: `vert_root`: each variable's matrix is the identity plus bounded noise. `tiles`: slot 0 of block row r is the identity plus bounded noise; the other slots are bounded noise. `level_reach`: level 0 uses 2 slots and the top level uses all 8; the count mostly rises with the level.
All inputs are finite; a program needn't handle non-finite values.
Results may differ from a plain program's by a relative error of at most 0.012.
Values may be sent and summed in bfloat16 or wider, within the bound.
No kernel may reach another device: no remote copies, remote signals or barrier semaphores. Data moves between devices by JAX's collectives and lax.ppermute only.
A program may use at most 128 MiB of HBM per device.

v0:
```python
import functools

import jax
import jax.numpy as jnp
from jax import lax
from jax.experimental import pallas as pl
from jax.experimental.pallas import tpu as pltpu
from jax.sharding import PartitionSpec as P


BF = jnp.bfloat16
F32 = jnp.float32
CORES = 2
FLOOR = 2
UNROLL = 8
LIFT_UNROLL = 4


def member_kernel(
    where_ref, cols_ref, ens_ref, mine_ref, other_ref, vt_ref, vn_ref, mask_ref, tiles_ref,
    near_ref, far_ref, ens_buf, tile_buf, lifted, spread_buf, ens_sems, tile_sems, *, var, slot_of_var,
):
    n_blocks, members, levels, width = ens_buf.shape
    y_n, z_n, x_n = mine_ref.shape[0], mine_ref.shape[1], mine_ref.shape[2]
    part_l = mine_ref.shape[4]
    slots = cols_ref.shape[1]
    my_y, my_z, my_x, my_c = where_ref[0], where_ref[1], where_ref[2], where_ref[3]
    n_copies = z_n
    per_copy = n_blocks // n_copies

    def ens_copy(off_z):
        span = pl.ds(lax.bitwise_xor(my_z, off_z) * per_copy, per_copy)
        return pltpu.make_async_copy(
            ens_ref.at[span, :, slot_of_var], ens_buf.at[span], ens_sems.at[off_z]
        )

    def tile_copy(piece):
        span = pl.ds(piece * per_copy, per_copy)
        return pltpu.make_async_copy(tiles_ref.at[span], tile_buf.at[span], tile_sems.at[piece])

    for piece in range(n_copies):
        ens_copy(piece).start()
    for piece in range(n_copies):
        tile_copy(piece).start()

    def seat_of(step):
        off_z, off_x = step // x_n, step % x_n
        z = lax.bitwise_xor(my_z, off_z)
        x = lax.bitwise_xor(my_x, off_x)
        return off_z, off_x, (z * x_n + x) * CORES

    def lift_block(source_ref, block, off_z, off_x):
        halves = []
        for m in range(members):
            bands = []
            for quarter in range(y_n):
                off_y = lax.bitwise_xor(my_y, quarter)
                incr = source_ref[off_y, off_z, off_x, var].astype(F32)
                rows = ens_buf[block, m, quarter * part_l:(quarter + 1) * part_l, :]
                bands.append((rows.astype(F32) * incr).astype(BF))
            halves.append(jnp.concatenate(bands, axis=0))
        weighted = jnp.concatenate(halves, axis=1)
        lift = jnp.dot(vt_ref[var], weighted, preferred_element_type=F32).astype(BF)
        for m in range(members):
            lifted[block, :, m * levels:(m + 1) * levels] = jnp.swapaxes(
                lift[:, m * width:(m + 1) * width], 0, 1
            )

    def lift_step(step, carry):
        off_z, off_x, base = seat_of(step)
        lift_block(mine_ref, base + my_c, off_z, off_x)
        lift_block(other_ref, base + 1 - my_c, off_z, off_x)
        return carry

    for off_z in range(z_n):
        ens_copy(off_z).wait()
        lax.fori_loop(off_z * x_n, (off_z + 1) * x_n, lift_step, 0, unroll=LIFT_UNROLL)

    def spread_block(block):
        parts = []
        for slot in range(slots):
            picked = lifted[cols_ref[block, slot]]
            if slot >= FLOOR:
                picked = picked * mask_ref[slot - FLOOR]
            parts.append(picked)
        spread = jnp.dot(
            tile_buf[block], jnp.concatenate(parts, axis=0), preferred_element_type=F32
        ).astype(BF)
        for m in range(members):
            spread_buf[block, m * width:(m + 1) * width, :] = spread[:, m * levels:(m + 1) * levels]

    def spread_step(step, carry):
        spread_block(step)
        return carry

    for piece in range(n_copies):
        tile_copy(piece).wait()
        lax.fori_loop(piece * per_copy, (piece + 1) * per_copy, spread_step, 0, unroll=UNROLL)

    def lower_block(target_ref, block, off_z, off_x):
        beside = spread_buf[block]
        lowered = lax.dot_general(
            vn_ref[var], beside, (((1,), (1,)), ((), ())), preferred_element_type=F32
        )
        total = None
        for m in range(members):
            term = ens_buf[block, m].astype(F32) * lowered[:, m * width:(m + 1) * width]
            total = term if total is None else total + term
        total = total.astype(BF)
        for quarter in range(y_n):
            off_y = lax.bitwise_xor(my_y, quarter)
            target_ref[off_y, off_z, off_x] = total[quarter * part_l:(quarter + 1) * part_l, :]

    def lower_step(step, carry):
        off_z, off_x, base = seat_of(step)
        lower_block(near_ref, base + my_c, off_z, off_x)
        lower_block(far_ref, base + 1 - my_c, off_z, off_x)
        return carry

    lax.fori_loop(0, n_blocks // CORES, lower_step, 0, unroll=8)


def cut_kernel(source_ref, piece_ref, stage, in_sems, out_sems, *, low):
    parts = in_sems.shape[0]
    blocks, _, count = piece_ref.shape[:3]
    per = blocks // parts

    def fetch(i):
        span = pl.ds(i * per, per)
        return pltpu.make_async_copy(
            source_ref.at[span, :, pl.ds(low, count)], stage.at[span], in_sems.at[i]
        )

    def put(i):
        span = pl.ds(i * per, per)
        return pltpu.make_async_copy(stage.at[span], piece_ref.at[span], out_sems.at[i])

    for i in range(parts):
        fetch(i).start()
    for i in range(parts):
        fetch(i).wait()
        put(i).start()
    for i in range(parts):
        put(i).wait()


def on_device(
    ensemble, increment, vert_root, tiles, tile_col, level_reach, *, y_n, z_n, x_n
):
    columns = lax.axis_size("col")
    members_all = ensemble.shape[0] * lax.axis_size("mem")
    members = ensemble.shape[0] // columns
    n_var, levels, width = ensemble.shape[1:]
    part_l = increment.shape[1]
    slots = tiles.shape[1]
    col = lax.axis_index("col")
    my_y = lax.axis_index("mem")
    my_z, my_x, my_c = col // (x_n * CORES), (col // CORES) % x_n, col % CORES
    where = jnp.stack([my_y, my_z, my_x, my_c]).astype(jnp.int32)

    def seat(z, x, c):
        return (z * x_n + x) * CORES + c

    seats = [(z, x, c) for z in range(z_n) for x in range(x_n) for c in range(CORES)]

    def shift_y(a, s):
        return lax.ppermute(a, "mem", [(i, i ^ s) for i in range(y_n)])

    def shift_z(a, s):
        return lax.ppermute(a, "col", [(seat(*p), seat(p[0] ^ s, p[1], p[2])) for p in seats])

    def shift_x(a, s):
        return lax.ppermute(a, "col", [(seat(*p), seat(p[0], p[1] ^ s, p[2])) for p in seats])

    def swap(a):
        return lax.ppermute(a, "col", [(seat(*p), seat(p[0], p[1], 1 - p[2])) for p in seats])

    def collect(a, shift, n):
        return jnp.stack([a] + [shift(a, s) for s in range(1, n)])

    by_member = ensemble.reshape(columns, members, n_var, levels, width)
    groups = ((0, 1), (2,))
    pieces = [by_member[:, :, group[0]:group[-1] + 1] for group in groups]
    pieces[0] = pl.pallas_call(
        functools.partial(cut_kernel, low=groups[0][0]),
        out_shape=jax.ShapeDtypeStruct(pieces[0].shape, BF),
        in_specs=[pl.BlockSpec(memory_space=pl.ANY)],
        out_specs=pl.BlockSpec(memory_space=pl.ANY),
        scratch_shapes=[
            pltpu.VMEM(pieces[0].shape, BF),
            pltpu.SemaphoreType.DMA((8,)),
            pltpu.SemaphoreType.DMA((8,)),
        ],
        compiler_params=pltpu.CompilerParams(vmem_limit_bytes=60 << 20),
        name="cut",
    )(by_member)
    where_var = {
        var: (index, place) for index, group in enumerate(groups) for place, var in enumerate(group)
    }

    mine = collect(increment, shift_x, x_n)
    pieces[0], mine = lax.optimization_barrier((pieces[0], mine))
    mine = collect(mine, shift_z, z_n)
    arrived = [lax.all_to_all(pieces[0], "col", 0, 0)]
    mine, pieces[1], tiles = lax.optimization_barrier((mine, pieces[1], tiles))
    turned_tiles = jnp.transpose(tiles, (0, 3, 1, 2)).reshape(columns, width, slots * width)
    mine = collect(mine, shift_y, y_n)
    mine, turned_tiles = lax.optimization_barrier((mine, turned_tiles))
    other = swap(mine)
    pieces[1], arrived[0] = lax.optimization_barrier((pieces[1], arrived[0]))
    arrived.append(lax.all_to_all(pieces[1], "col", 0, 0))

    vert_t = jnp.swapaxes(vert_root, 1, 2)
    active = (
        jnp.arange(FLOOR, slots, dtype=jnp.int32)[:, None] < level_reach[None, :]
    ).astype(BF)
    mask = jnp.tile(active, (1, members))[:, None, :]

    vmem = pl.BlockSpec(memory_space=pltpu.VMEM)
    smem = pl.BlockSpec(memory_space=pltpu.SMEM)
    anywhere = pl.BlockSpec(memory_space=pl.ANY)
    out = jax.ShapeDtypeStruct((y_n, z_n, x_n, part_l, width), BF)

    def add(parts):
        total = parts[0].astype(F32)
        for p in parts[1:]:
            total = total + p.astype(F32)
        return total

    chips = []
    for var in range(n_var):
        index, place = where_var[var]
        if index and place == 0:
            early = jnp.stack(chips, axis=3)
            early = add([early[0]] + [shift_y(early[s], s) for s in range(1, y_n)]).astype(BF)
            chips = []
        near, far = pl.pallas_call(
            functools.partial(member_kernel, var=var, slot_of_var=place),
            out_shape=(out, out),
            in_specs=[smem, smem, anywhere, vmem, vmem, vmem, vmem, vmem,
                      anywhere],
            out_specs=(vmem, vmem),
            scratch_shapes=[
                pltpu.VMEM((columns, members, levels, width), BF),
                pltpu.VMEM(turned_tiles.shape, BF),
                pltpu.VMEM((columns, width, members * levels), BF),
                pltpu.VMEM((columns, members * width, levels), BF),
                pltpu.SemaphoreType.DMA((z_n,)),
                pltpu.SemaphoreType.DMA((z_n,)),
            ],
            compiler_params=pltpu.CompilerParams(vmem_limit_bytes=40 << 20),
        )(where, tile_col, arrived[index], mine, other, vert_t, vert_root, mask, turned_tiles)
        chips.append(add([near, swap(far)]).astype(BF))
    late = jnp.stack(chips, axis=3)
    late = add([late[0]] + [shift_y(late[s], s) for s in range(1, y_n)]).astype(BF)
    held = jnp.concatenate([early, late], axis=2)
    held = add([held[0]] + [shift_z(held[s], s) for s in range(1, z_n)]).astype(BF)
    held = add([held[0]] + [shift_x(held[s], s) for s in range(1, x_n)])
    return (held / (members_all - 1)).astype(BF)


def solution(mesh):
    y_n = mesh.shape["mem"]
    side = int(round((mesh.shape["col"] // CORES) ** 0.5))
    placed = (P("mem", None, None, "col"), P(None, "mem", "col"), P(), P(), P(), P())
    return jax.shard_map(
        functools.partial(on_device, y_n=y_n, z_n=side, x_n=side),
        mesh=mesh, in_specs=placed, out_specs=P(None, "mem", "col"), check_vma=False,
    )
```

profile of v0, /device:TPU:0, one launch (start us, length us, event | category | flops | bytes accessed | tf_op | source)
XLA Modules:
  0.0 175.5 jit_solution(9214639486366089405)
XLA Ops:
  0.0 1.6 collective-permute-start
  1.6 2.1 %collective-permute-start.2 = (bf16[3,32,128]{2,1,0:T(8,128)(2,1)}, bf16[3,32,128]{2,1,0:T(8,128)(2,1)S(1)}, u32[]{:S(2)}, u32[]{:S(2)}) collective-permute-start(bf16[3,32,128]{2,1,0:T(8,128)(2,1)} %param.7), channel_id=1, source_target_pairs={{0,6},{1,7},{2,4},{3,5},{4,2},{5,3},{6,0},{7,1},{8,14},{9,15},{10,... | collective-permute-start | bytes 73736 | tf_op jit(solution)/shard_map/ppermute | solution.py:173
  4.3 3.6 %cut.1 = bf16[32,2,2,128,128]{4,3,2,1,0:T(8,128)(2,1)} custom-call(bf16[32,2,3,128,128]{4,3,2,1,0:T(8,128)(2,1)} %bitcast.90), custom_call_target="tpu_custom_call" | custom-call | tf_op jit(solution)/shard_map/cut/pallas_call | solution.py:184
  9.3 6.9 %all-to-all-start = ((bf16[32,2,2,128,128]{4,3,2,1,0:T(8,128)(2,1)}), bf16[32,2,2,128,128]{4,3,2,1,0:T(8,128)(2,1)}, u32[]{:S(2)}, u32[]{:S(2)}) async-start(bf16[32,2,2,128,128]{4,3,2,1,0:T(8,128)(2,1)} %cut.1), calls=%async_computation | async-start | bytes 8388608 | tf_op jit(solution)/shard_map/all_to_all | solution.py:204
  16.2 3.1 %collective-permute-start.5 = (bf16[4,3,32,128]{3,2,1,0:T(8,128)(2,1)S(1)}, bf16[4,3,32,128]{3,2,1,0:T(8,128)(2,1)S(1)}, u32[]{:S(2)}, u32[]{:S(2)}) collective-permute-start(bf16[4,3,32,128]{3,2,1,0:T(8,128)(2,1)S(1)} %pad_maximum_fusion.4), channel_id=1, source_target_pairs={{0,24},{1,25},{2,26},{3,27},{4,28},{5,29},{6,30},{7,31},{8,16},{9,... | collective-permute-start | bytes 294920 | tf_op jit(solution)/shard_map/ppermute | solution.py:170
  20.4 3.2 %slice.72 = bf16[32,2,1,128,128]{4,3,2,1,0:T(8,128)(2,1)} slice(bf16[32,2,3,128,128]{4,3,2,1,0:T(8,128)(2,1)} %bitcast.91), slice={[0:32], [0:2], [2:3], [0:128], [0:128]} | slice | bytes 4194304 | tf_op jit(solution)/shard_map/slice | solution.py:183
  23.6 45.0 %collective-permute-done.5 = bf16[4,3,32,128]{3,2,1,0:T(8,128)(2,1)S(1)} collective-permute-done((bf16[4,3,32,128]{3,2,1,0:T(8,128)(2,1)S(1)}, bf16[4,3,32,128]{3,2,1,0:T(8,128)(2,1)S(1)}, u32[]{:S(2)}, u32[]{:S(2)}) %collective-permute-start.5) | collective-permute-done | bytes 98336 | tf_op jit(solution)/shard_map/ppermute | solution.py:170
  68.6 3.1 %collective-permute-start.8 = (bf16[4,4,3,32,128]{4,3,2,1,0:T(8,128)(2,1)S(1)}, bf16[4,4,3,32,128]{4,3,2,1,0:T(8,128)(2,1)S(1)}, u32[]{:S(2)}, u32[]{:S(2)}) collective-permute-start(bf16[4,4,3,32,128]{4,3,2,1,0:T(8,128)(2,1)S(1)} %pad_maximum_fusion.1), channel_id=1, source_target_pairs={{0,96},{32,64},{64,32},{96,0},{1,97},{33,65},{65,33},{97,1},{2,98}... | collective-permute-start | bytes 1179656 | tf_op jit(solution)/shard_map/ppermute | solution.py:167
  72.8 11.9 %copy.38.tiles_ref = bf16[32,128,1024]{2,1,0:T(8,128)(2,1)} copy(bf16[32,128,1024]{1,2,0:T(8,128)(2,1)} %bitcast.92) | data formatting | bytes 16777216 | tf_op jit(solution)/shard_map/reshape | solution.py:206
  84.8 4.3 %collective-permute-done.8 = bf16[4,4,3,32,128]{4,3,2,1,0:T(8,128)(2,1)S(1)} collective-permute-done((bf16[4,4,3,32,128]{4,3,2,1,0:T(8,128)(2,1)S(1)}, bf16[4,4,3,32,128]{4,3,2,1,0:T(8,128)(2,1)S(1)}, u32[]{:S(2)}, u32[]{:S(2)}) %collective-permute-start.8) | collective-permute-done | bytes 393248 | tf_op jit(solution)/shard_map/ppermute | solution.py:167
  90.1 6.7 %all-to-all-start.1 = ((bf16[32,2,1,128,128]{4,3,2,1,0:T(8,128)(2,1)}), bf16[32,2,1,128,128]{4,3,2,1,0:T(8,128)(2,1)}, u32[]{:S(2)}, u32[]{:S(2)}) async-start(bf16[32,2,1,128,128]{4,3,2,1,0:T(8,128)(2,1)} %slice.72), calls=%async_computation.1 | async-start | bytes 4194304 | tf_op jit(solution)/shard_map/all_to_all | solution.py:211
  97.3 9.2 %shard_map.65 = (bf16[4,4,4,32,128]{4,3,2,1,0:T(8,128)(2,1)S(1)}, bf16[4,4,4,32,128]{4,3,2,1,0:T(8,128)(2,1)}) custom-call(s32[4]{0:T(128)S(1)} %pad_add_fusion.where_ref, s32[32,8]{1,0:T(8,128)S(1)} %copy.23.cols_ref, bf16[32,2,2,128,128]{4,3,2,1,0:T(8,128)(2,1)} %all-to-all-done.ens_ref, bf16[4,4,4,3,32,128]{5,4,3,2,1,0:T(8,128)(2,1)S(1)} %pad_maximum_fusion.mine_ref, ...), custom_call_target="tpu_custom_call" | custom-call | tf_op jit(solution)/shard_map/pallas_call | solution.py:237
  107.5 9.2 %shard_map.64 = (bf16[4,4,4,32,128]{4,3,2,1,0:T(8,128)(2,1)S(1)}, bf16[4,4,4,32,128]{4,3,2,1,0:T(8,128)(2,1)}) custom-call(s32[4]{0:T(128)S(1)} %pad_add_fusion.where_ref, s32[32,8]{1,0:T(8,128)S(1)} %copy.23.cols_ref, bf16[32,2,2,128,128]{4,3,2,1,0:T(8,128)(2,1)} %all-to-all-done.ens_ref, bf16[4,4,4,3,32,128]{5,4,3,2,1,0:T(8,128)(2,1)S(1)} %pad_maximum_fusion.mine_ref, ...), custom_call_target="tpu_custom_call" | custom-call | tf_op jit(solution)/shard_map/pallas_call | solution.py:237
  117.8 9.0 %all-to-all-done.1.ens_ref = bf16[32,2,1,128,128]{4,3,2,1,0:T(8,128)(2,1)} async-done(((bf16[32,2,1,128,128]{4,3,2,1,0:T(8,128)(2,1)}), bf16[32,2,1,128,128]{4,3,2,1,0:T(8,128)(2,1)}, u32[]{:S(2)}, u32[]{:S(2)}) %all-to-all-start.1) | async-done | bytes 2097184 | tf_op jit(solution)/shard_map/all_to_all | solution.py:211
  126.8 8.4 %shard_map.66 = (bf16[4,4,4,32,128]{4,3,2,1,0:T(8,128)(2,1)S(1)}, bf16[4,4,4,32,128]{4,3,2,1,0:T(8,128)(2,1)S(1)}) custom-call(s32[4]{0:T(128)S(1)} %pad_add_fusion.where_ref, s32[32,8]{1,0:T(8,128)S(1)} %copy.23.cols_ref, bf16[32,2,1,128,128]{4,3,2,1,0:T(8,128)(2,1)} %all-to-all-done.1.ens_ref, ...), custom_call_target="tpu_custom_call" | custom-call | tf_op jit(solution)/shard_map/pallas_call | solution.py:237
  139.4 2.2 %collective-permute-start.14 = (bf16[4,4,2,32,128]{4,3,1,0,2:T(8,128)(2,1)S(1)}, bf16[4,4,2,32,128]{4,3,1,0,2:T(8,128)(2,1)S(1)}, u32[]{:S(2)}, u32[]{:S(2)}) collective-permute-start(bf16[4,4,2,32,128]{4,3,1,0,2:T(8,128)(2,1)S(1)} %get-tuple-element.36), channel_id=1, source_target_pairs={{0,96},{32,64},{64,32},{96,0},{1,97},{33,65},{65,33},{97,1},{2,98}... | collective-permute-start | bytes 786440 | tf_op jit(solution)/shard_map/ppermute | solution.py:167
  143.8 2.2 %collective-permute-start.18 = (bf16[4,4,1,32,128]{4,3,1,0,2:T(8,128)(2,1)S(1)}, bf16[4,4,1,32,128]{4,3,1,0,2:T(8,128)(2,1)S(1)}, u32[]{:S(2)}, u32[]{:S(2)}) collective-permute-start(bf16[4,4,1,32,128]{4,3,1,0,2:T(8,128)(2,1)S(1)} %get-tuple-element.39), channel_id=1, source_target_pairs={{0,96},{32,64},{64,32},{96,0},{1,97},{33,65},{65,33},{97,1},{2,98}... | collective-permute-start | bytes 393224 | tf_op jit(solution)/shard_map/ppermute | solution.py:167
  147.1 3.0 %collective-permute-start.17 = (bf16[4,4,1,32,128]{4,3,1,0,2:T(8,128)(2,1)S(1)}, bf16[4,4,1,32,128]{4,3,1,0,2:T(8,128)(2,1)S(1)}, u32[]{:S(2)}, u32[]{:S(2)}) collective-permute-start(bf16[4,4,1,32,128]{4,3,1,0,2:T(8,128)(2,1)S(1)} %get-tuple-element.40), channel_id=1, source_target_pairs={{0,64},{32,96},{64,0},{96,32},{1,65},{33,97},{65,1},{97,33},{2,66}... | collective-permute-start | bytes 393224 | tf_op jit(solution)/shard_map/ppermute | solution.py:167
  150.2 5.2 %collective-permute-done.14 = bf16[4,4,2,32,128]{4,3,1,0,2:T(8,128)(2,1)S(1)} collective-permute-done((bf16[4,4,2,32,128]{4,3,1,0,2:T(8,128)(2,1)S(1)}, bf16[4,4,2,32,128]{4,3,1,0,2:T(8,128)(2,1)S(1)}, u32[]{:S(2)}, u32[]{:S(2)}) %collective-permute-start.14) | collective-permute-done | bytes 262176 | tf_op jit(solution)/shard_map/ppermute | solution.py:167
  155.6 3.1 %collective-permute-done.18 = bf16[4,4,1,32,128]{4,3,1,0,2:T(8,128)(2,1)S(1)} collective-permute-done((bf16[4,4,1,32,128]{4,3,1,0,2:T(8,128)(2,1)S(1)}, bf16[4,4,1,32,128]{4,3,1,0,2:T(8,128)(2,1)S(1)}, u32[]{:S(2)}, u32[]{:S(2)}) %collective-permute-start.18) | collective-permute-done | bytes 131104 | tf_op jit(solution)/shard_map/ppermute | solution.py:167
  160.4 1.7 collective-permute-start.21
  162.1 2.4 %collective-permute-start.20 = (bf16[4,3,32,128]{3,2,0,1:T(8,128)(2,1)S(1)}, bf16[4,3,32,128]{3,2,0,1:T(8,128)(2,1)S(1)}, u32[]{:S(2)}, u32[]{:S(2)}) collective-permute-start(bf16[4,3,32,128]{3,2,0,1:T(8,128)(2,1)S(1)} %get-tuple-element.43), channel_id=1, source_target_pairs={{0,16},{1,17},{2,18},{3,19},{4,20},{5,21},{6,22},{7,23},{8,24},{9,... | collective-permute-start | bytes 294920 | tf_op jit(solution)/shard_map/ppermute | solution.py:170
  165.6 2.7 %collective-permute-done.21 = bf16[4,3,32,128]{3,2,0,1:T(8,128)(2,1)S(1)} collective-permute-done((bf16[4,3,32,128]{3,2,0,1:T(8,128)(2,1)S(1)}, bf16[4,3,32,128]{3,2,0,1:T(8,128)(2,1)S(1)}, u32[]{:S(2)}, u32[]{:S(2)}) %collective-permute-start.21) | collective-permute-done | bytes 98336 | tf_op jit(solution)/shard_map/ppermute | solution.py:170
  169.5 3.0 %collective-permute-start.23 = (bf16[3,32,128]{2,1,0:T(8,128)(2,1)S(1)}, bf16[3,32,128]{2,1,0:T(8,128)(2,1)S(1)}, u32[]{:S(2)}, u32[]{:S(2)}) collective-permute-start(bf16[3,32,128]{2,1,0:T(8,128)(2,1)S(1)} %get-tuple-element.46), channel_id=1, source_target_pairs={{0,4},{1,5},{2,6},{3,7},{4,0},{5,1},{6,2},{7,3},{8,12},{9,13},{10,... | collective-permute-start | bytes 73736 | tf_op jit(solution)/shard_map/ppermute | solution.py:173
  (73 shorter events, 22.3 us)
Async XLA Ops:
  0.0 7.9 %collective-permute-start = (bf16[3,32,128]{2,1,0:T(8,128)(2,1)}, bf16[3,32,128]{2,1,0:T(8,128)(2,1)S(1)}, u32[]{:S(2)}, u32[]{:S(2)}) collective-permute-start(bf16[3,32,128]{2,1,0:T(8,128)(2,1)} %param.7), channel_id=1, source_target_pairs={{0,2},{1,3},{2,0},{3,1},{4,6},{5,7},{6,4},{7,5},{8,10},{9,11},{10,... | collective-permute-start | bytes 73736 | tf_op jit(solution)/shard_map/ppermute | solution.py:173
  1.6 6.3 %collective-permute-start.2 = (bf16[3,32,128]{2,1,0:T(8,128)(2,1)}, bf16[3,32,128]{2,1,0:T(8,128)(2,1)S(1)}, u32[]{:S(2)}, u32[]{:S(2)}) collective-permute-start(bf16[3,32,128]{2,1,0:T(8,128)(2,1)} %param.7), channel_id=1, source_target_pairs={{0,6},{1,7},{2,4},{3,5},{4,2},{5,3},{6,0},{7,1},{8,14},{9,15},{10,... | collective-permute-start | bytes 73736 | tf_op jit(solution)/shard_map/ppermute | solution.py:173
  3.7 5.5 %collective-permute-start.1 = (bf16[3,32,128]{2,1,0:T(8,128)(2,1)}, bf16[3,32,128]{2,1,0:T(8,128)(2,1)S(1)}, u32[]{:S(2)}, u32[]{:S(2)}) collective-permute-start(bf16[3,32,128]{2,1,0:T(8,128)(2,1)} %param.7), channel_id=1, source_target_pairs={{0,4},{1,5},{2,6},{3,7},{4,0},{5,1},{6,2},{7,3},{8,12},{9,13},{10,... | collective-permute-start | bytes 73736 | tf_op jit(solution)/shard_map/ppermute | solution.py:173
  9.3 80.8 %all-to-all-start = ((bf16[32,2,2,128,128]{4,3,2,1,0:T(8,128)(2,1)}), bf16[32,2,2,128,128]{4,3,2,1,0:T(8,128)(2,1)}, u32[]{:S(2)}, u32[]{:S(2)}) async-start(bf16[32,2,2,128,128]{4,3,2,1,0:T(8,128)(2,1)} %cut.1), calls=%async_computation | async-start | bytes 8388608 | tf_op jit(solution)/shard_map/all_to_all | solution.py:204
  16.2 52.4 %collective-permute-start.5 = (bf16[4,3,32,128]{3,2,1,0:T(8,128)(2,1)S(1)}, bf16[4,3,32,128]{3,2,1,0:T(8,128)(2,1)S(1)}, u32[]{:S(2)}, u32[]{:S(2)}) collective-permute-start(bf16[4,3,32,128]{3,2,1,0:T(8,128)(2,1)S(1)} %pad_maximum_fusion.4), channel_id=1, source_target_pairs={{0,24},{1,25},{2,26},{3,27},{4,28},{5,29},{6,30},{7,31},{8,16},{9,... | collective-permute-start | bytes 294920 | tf_op jit(solution)/shard_map/ppermute | solution.py:170
  19.2 49.4 %collective-permute-start.4 = (bf16[4,3,32,128]{3,2,1,0:T(8,128)(2,1)S(1)}, bf16[4,3,32,128]{3,2,1,0:T(8,128)(2,1)S(1)}, u32[]{:S(2)}, u32[]{:S(2)}) collective-permute-start(bf16[4,3,32,128]{3,2,1,0:T(8,128)(2,1)S(1)} %pad_maximum_fusion.4), channel_id=1, source_target_pairs={{0,16},{1,17},{2,18},{3,19},{4,20},{5,21},{6,22},{7,23},{8,24},{9,... | collective-permute-start | bytes 294920 | tf_op jit(solution)/shard_map/ppermute | solution.py:170
  20.0 48.5 %collective-permute-start.3 = (bf16[4,3,32,128]{3,2,1,0:T(8,128)(2,1)S(1)}, bf16[4,3,32,128]{3,2,1,0:T(8,128)(2,1)S(1)}, u32[]{:S(2)}, u32[]{:S(2)}) collective-permute-start(bf16[4,3,32,128]{3,2,1,0:T(8,128)(2,1)S(1)} %pad_maximum_fusion.4), channel_id=1, source_target_pairs={{0,8},{1,9},{2,10},{3,11},{4,12},{5,13},{6,14},{7,15},{8,0},{9,1},... | collective-permute-start | bytes 294920 | tf_op jit(solution)/shard_map/ppermute | solution.py:170
  68.6 20.4 %collective-permute-start.8 = (bf16[4,4,3,32,128]{4,3,2,1,0:T(8,128)(2,1)S(1)}, bf16[4,4,3,32,128]{4,3,2,1,0:T(8,128)(2,1)S(1)}, u32[]{:S(2)}, u32[]{:S(2)}) collective-permute-start(bf16[4,4,3,32,128]{4,3,2,1,0:T(8,128)(2,1)S(1)} %pad_maximum_fusion.1), channel_id=1, source_target_pairs={{0,96},{32,64},{64,32},{96,0},{1,97},{33,65},{65,33},{97,1},{2,98}... | collective-permute-start | bytes 1179656 | tf_op jit(solution)/shard_map/ppermute | solution.py:167
  71.7 17.3 %collective-permute-start.7 = (bf16[4,4,3,32,128]{4,3,2,1,0:T(8,128)(2,1)S(1)}, bf16[4,4,3,32,128]{4,3,2,1,0:T(8,128)(2,1)S(1)}, u32[]{:S(2)}, u32[]{:S(2)}) collective-permute-start(bf16[4,4,3,32,128]{4,3,2,1,0:T(8,128)(2,1)S(1)} %pad_maximum_fusion.1), channel_id=1, source_target_pairs={{0,64},{32,96},{64,0},{96,32},{1,65},{33,97},{65,1},{97,33},{2,66}... | collective-permute-start | bytes 1179656 | tf_op jit(solution)/shard_map/ppermute | solution.py:167
  72.4 17.4 %collective-permute-start.6 = (bf16[4,4,3,32,128]{4,3,2,1,0:T(8,128)(2,1)S(1)}, bf16[4,4,3,32,128]{4,3,2,1,0:T(8,128)(2,1)S(1)}, u32[]{:S(2)}, u32[]{:S(2)}) collective-permute-start(bf16[4,4,3,32,128]{4,3,2,1,0:T(8,128)(2,1)S(1)} %pad_maximum_fusion.1), channel_id=1, source_target_pairs={{0,32},{32,0},{64,96},{96,64},{1,33},{33,1},{65,97},{97,65},{2,34}... | collective-permute-start | bytes 1179656 | tf_op jit(solution)/shard_map/ppermute | solution.py:167
  90.0 7.3 %collective-permute-start.9 = (bf16[4,4,4,3,32,128]{5,4,3,2,1,0:T(8,128)(2,1)S(1)}, bf16[4,4,4,3,32,128]{5,4,3,2,1,0:T(8,128)(2,1)S(1)}, u32[]{:S(2)}, u32[]{:S(2)}) collective-permute-start(bf16[4,4,4,3,32,128]{5,4,3,2,1,0:T(8,128)(2,1)S(1)} %pad_maximum_fusion.mine_ref), channel_id=1, source_target_pairs={{0,1},{1,0},{2,3},{3,2},{4,5},{5,4},{6,7},{7,6},{8,9},{9,8},{10,11... | collective-permute-start | bytes 4718600 | tf_op jit(solution)/shard_map/ppermute | solution.py:176
  90.1 36.8 %all-to-all-start.1 = ((bf16[32,2,1,128,128]{4,3,2,1,0:T(8,128)(2,1)}), bf16[32,2,1,128,128]{4,3,2,1,0:T(8,128)(2,1)}, u32[]{:S(2)}, u32[]{:S(2)}) async-start(bf16[32,2,1,128,128]{4,3,2,1,0:T(8,128)(2,1)} %slice.72), calls=%async_computation.1 | async-start | bytes 4194304 | tf_op jit(solution)/shard_map/all_to_all | solution.py:211
  107.3 28.0 %collective-permute-start.11 = (bf16[4,4,4,32,128]{4,3,2,1,0:T(8,128)(2,1)}, bf16[4,4,4,32,128]{4,3,2,1,0:T(8,128)(2,1)}, u32[]{:S(2)}, u32[]{:S(2)}) collective-permute-start(bf16[4,4,4,32,128]{4,3,2,1,0:T(8,128)(2,1)} %get-tuple-element.31), channel_id=1, source_target_pairs={{0,1},{1,0},{2,3},{3,2},{4,5},{5,4},{6,7},{7,6},{8,9},{9,8},{10,11... | collective-permute-start | bytes 1572872 | tf_op jit(solution)/shard_map/ppermute | solution.py:176
  117.5 19.1 %collective-permute-start.10 = (bf16[4,4,4,32,128]{4,3,2,1,0:T(8,128)(2,1)}, bf16[4,4,4,32,128]{4,3,2,1,0:T(8,128)(2,1)}, u32[]{:S(2)}, u32[]{:S(2)}) collective-permute-start(bf16[4,4,4,32,128]{4,3,2,1,0:T(8,128)(2,1)} %get-tuple-element.29), channel_id=1, source_target_pairs={{0,1},{1,0},{2,3},{3,2},{4,5},{5,4},{6,7},{7,6},{8,9},{9,8},{10,11... | collective-permute-start | bytes 1572872 | tf_op jit(solution)/shard_map/ppermute | solution.py:176
  135.2 7.1 %collective-permute-start.15 = (bf16[4,4,4,32,128]{4,3,2,1,0:T(8,128)(2,1)S(1)}, bf16[4,4,4,32,128]{4,3,2,1,0:T(8,128)(2,1)S(1)}, u32[]{:S(2)}, u32[]{:S(2)}) collective-permute-start(bf16[4,4,4,32,128]{4,3,2,1,0:T(8,128)(2,1)S(1)} %get-tuple-element.34), channel_id=1, source_target_pairs={{0,1},{1,0},{2,3},{3,2},{4,5},{5,4},{6,7},{7,6},{8,9},{9,8},{10,11... | collective-permute-start | bytes 1572872 | tf_op jit(solution)/shard_map/ppermute | solution.py:176
  137.9 9.3 %collective-permute-start.12 = (bf16[4,4,2,32,128]{4,3,1,0,2:T(8,128)(2,1)S(1)}, bf16[4,4,2,32,128]{4,3,1,0,2:T(8,128)(2,1)S(1)}, u32[]{:S(2)}, u32[]{:S(2)}) collective-permute-start(bf16[4,4,2,32,128]{4,3,1,0,2:T(8,128)(2,1)S(1)} %get-tuple-element.35), channel_id=1, source_target_pairs={{0,32},{32,0},{64,96},{96,64},{1,33},{33,1},{65,97},{97,65},{2,34}... | collective-permute-start | bytes 786440 | tf_op jit(solution)/shard_map/ppermute | solution.py:167
  139.4 16.0 %collective-permute-start.14 = (bf16[4,4,2,32,128]{4,3,1,0,2:T(8,128)(2,1)S(1)}, bf16[4,4,2,32,128]{4,3,1,0,2:T(8,128)(2,1)S(1)}, u32[]{:S(2)}, u32[]{:S(2)}) collective-permute-start(bf16[4,4,2,32,128]{4,3,1,0,2:T(8,128)(2,1)S(1)} %get-tuple-element.36), channel_id=1, source_target_pairs={{0,96},{32,64},{64,32},{96,0},{1,97},{33,65},{65,33},{97,1},{2,98}... | collective-permute-start | bytes 786440 | tf_op jit(solution)/shard_map/ppermute | solution.py:167
  141.6 13.8 %collective-permute-start.13 = (bf16[4,4,2,32,128]{4,3,1,0,2:T(8,128)(2,1)S(1)}, bf16[4,4,2,32,128]{4,3,1,0,2:T(8,128)(2,1)S(1)}, u32[]{:S(2)}, u32[]{:S(2)}) collective-permute-start(bf16[4,4,2,32,128]{4,3,1,0,2:T(8,128)(2,1)S(1)} %get-tuple-element.37), channel_id=1, source_target_pairs={{0,64},{32,96},{64,0},{96,32},{1,65},{33,97},{65,1},{97,33},{2,66}... | collective-permute-start | bytes 786440 | tf_op jit(solution)/shard_map/ppermute | solution.py:167
  142.5 13.1 %collective-permute-start.16 = (bf16[4,4,1,32,128]{4,3,1,0,2:T(8,128)(2,1)S(1)}, bf16[4,4,1,32,128]{4,3,1,0,2:T(8,128)(2,1)S(1)}, u32[]{:S(2)}, u32[]{:S(2)}) collective-permute-start(bf16[4,4,1,32,128]{4,3,1,0,2:T(8,128)(2,1)S(1)} %get-tuple-element.38), channel_id=1, source_target_pairs={{0,32},{32,0},{64,96},{96,64},{1,33},{33,1},{65,97},{97,65},{2,34}... | collective-permute-start | bytes 393224 | tf_op jit(solution)/shard_map/ppermute | solution.py:167
  143.8 14.9 %collective-permute-start.18 = (bf16[4,4,1,32,128]{4,3,1,0,2:T(8,128)(2,1)S(1)}, bf16[4,4,1,32,128]{4,3,1,0,2:T(8,128)(2,1)S(1)}, u32[]{:S(2)}, u32[]{:S(2)}) collective-permute-start(bf16[4,4,1,32,128]{4,3,1,0,2:T(8,128)(2,1)S(1)} %get-tuple-element.39), channel_id=1, source_target_pairs={{0,96},{32,64},{64,32},{96,0},{1,97},{33,65},{65,33},{97,1},{2,98}... | collective-permute-start | bytes 393224 | tf_op jit(solution)/shard_map/ppermute | solution.py:167
  147.1 13.1 %collective-permute-start.17 = (bf16[4,4,1,32,128]{4,3,1,0,2:T(8,128)(2,1)S(1)}, bf16[4,4,1,32,128]{4,3,1,0,2:T(8,128)(2,1)S(1)}, u32[]{:S(2)}, u32[]{:S(2)}) collective-permute-start(bf16[4,4,1,32,128]{4,3,1,0,2:T(8,128)(2,1)S(1)} %get-tuple-element.40), channel_id=1, source_target_pairs={{0,64},{32,96},{64,0},{96,32},{1,65},{33,97},{65,1},{97,33},{2,66}... | collective-permute-start | bytes 393224 | tf_op jit(solution)/shard_map/ppermute | solution.py:167
  160.4 7.9 %collective-permute-start.21 = (bf16[4,3,32,128]{3,2,0,1:T(8,128)(2,1)S(1)}, bf16[4,3,32,128]{3,2,0,1:T(8,128)(2,1)S(1)}, u32[]{:S(2)}, u32[]{:S(2)}) collective-permute-start(bf16[4,3,32,128]{3,2,0,1:T(8,128)(2,1)S(1)} %get-tuple-element.42), channel_id=1, source_target_pairs={{0,24},{1,25},{2,26},{3,27},{4,28},{5,29},{6,30},{7,31},{8,16},{9,... | collective-permute-start | bytes 294920 | tf_op jit(solution)/shard_map/ppermute | solution.py:170
  162.1 6.2 %collective-permute-start.20 = (bf16[4,3,32,128]{3,2,0,1:T(8,128)(2,1)S(1)}, bf16[4,3,32,128]{3,2,0,1:T(8,128)(2,1)S(1)}, u32[]{:S(2)}, u32[]{:S(2)}) collective-permute-start(bf16[4,3,32,128]{3,2,0,1:T(8,128)(2,1)S(1)} %get-tuple-element.43), channel_id=1, source_target_pairs={{0,16},{1,17},{2,18},{3,19},{4,20},{5,21},{6,22},{7,23},{8,24},{9,... | collective-permute-start | bytes 294920 | tf_op jit(solution)/shard_map/ppermute | solution.py:170
  169.5 5.3 %collective-permute-start.23 = (bf16[3,32,128]{2,1,0:T(8,128)(2,1)S(1)}, bf16[3,32,128]{2,1,0:T(8,128)(2,1)S(1)}, u32[]{:S(2)}, u32[]{:S(2)}) collective-permute-start(bf16[3,32,128]{2,1,0:T(8,128)(2,1)S(1)} %get-tuple-element.46), channel_id=1, source_target_pairs={{0,4},{1,5},{2,6},{3,7},{4,0},{5,1},{6,2},{7,3},{8,12},{9,13},{10,... | collective-permute-start | bytes 73736 | tf_op jit(solution)/shard_map/ppermute | solution.py:173
  (11 other events, 52.0 us)
where the time goes:
time: 176 us; the launch traced here: 175 us
  waiting for transfers between devices  77.5 us (44%)
  starting transfers between devices  46.2 us (26%)
  Pallas kernels  30.3 us (17%)
  local copies, waits for them, and re-layouts  17 us (10%)
  other arithmetic  4 us (2%)
    ppermute x6, waiting for transfers between devices, shift_z(): lax.ppermute(a, 'col', [(seat(*p), seat(p[0] ^ s, p[1], p[2])) for p in s...  48.8 us
    pallas_call x3, Pallas kernels, on_device(): pl.pallas_call(functools.partial(member_kernel, var=var, slot_of_var=plac...  26.8 us
    ppermute x9, waiting for transfers between devices, shift_y(): return lax.ppermute(a, 'mem', [(i, i ^ s) for i in range(y_n)])  16 us
    ppermute x9, starting transfers between devices, shift_y(): return lax.ppermute(a, 'mem', [(i, i ^ s) for i in range(y_n)])  15.1 us
    reshape x1, local copies, waits for them, and re-layouts, on_device(): jnp.transpose(tiles, (0, 3, 1, 2)).reshape(columns, width, slots * width)  11.9 us
    all_to_all x1, waiting for transfers between devices, on_device(): arrived.append(lax.all_to_all(pieces[1], 'col', 0, 0))  9.03 us
    ppermute x6, starting transfers between devices, shift_x(): lax.ppermute(a, 'col', [(seat(*p), seat(p[0], p[1] ^ s, p[2])) for p in s...  8.5 us
    ppermute x6, starting transfers between devices, shift_z(): lax.ppermute(a, 'col', [(seat(*p), seat(p[0] ^ s, p[1], p[2])) for p in s...  8.34 us
  transfers between devices with their start and end apart: 27, of which 14 were waited for; matrix products, arithmetic and copies ran while one was open for 11% of the time, Pallas kernels for 17%

commit v1 on v0

--- a/solution.py
+++ b/solution.py
@@ -118,6 +118,10 @@
         return carry
 
     lax.fori_loop(0, n_blocks // CORES, lower_step, 0, unroll=8)
+
+
+def far_first(n):
+    return sorted(range(1, n), key=lambda s: (s != n // 2, -s))
 
 
 def cut_kernel(source_ref, piece_ref, stage, in_sems, out_sems, *, low):
@@ -176,7 +180,8 @@
         return lax.ppermute(a, "col", [(seat(*p), seat(p[0], p[1], 1 - p[2])) for p in seats])
 
     def collect(a, shift, n):
-        return jnp.stack([a] + [shift(a, s) for s in range(1, n)])
+        got = {s: shift(a, s) for s in far_first(n)}
+        return jnp.stack([a] + [got[s] for s in range(1, n)])
 
     by_member = ensemble.reshape(columns, members, n_var, levels, width)
     groups = ((0, 1), (2,))
@@ -232,7 +237,7 @@
         index, place = where_var[var]
         if index and place == 0:
             early = jnp.stack(chips, axis=3)
-            early = add([early[0]] + [shift_y(early[s], s) for s in range(1, y_n)]).astype(BF)
+            early = add([early[0]] + [shift_y(early[s], s) for s in far_first(y_n)]).astype(BF)
             chips = []
         near, far = pl.pallas_call(
             functools.partial(member_kernel, var=var, slot_of_var=place),
@@ -252,10 +257,10 @@
         )(where, tile_col, arrived[index], mine, other, vert_t, vert_root, mask, turned_tiles)
         chips.append(add([near, swap(far)]).astype(BF))
     late = jnp.stack(chips, axis=3)
-    late = add([late[0]] + [shift_y(late[s], s) for s in range(1, y_n)]).astype(BF)
+    late = add([late[0]] + [shift_y(late[s], s) for s in far_first(y_n)]).astype(BF)
     held = jnp.concatenate([early, late], axis=2)
-    held = add([held[0]] + [shift_z(held[s], s) for s in range(1, z_n)]).astype(BF)
-    held = add([held[0]] + [shift_x(held[s], s) for s in range(1, x_n)])
+    held = add([held[0]] + [shift_z(held[s], s) for s in far_first(z_n)]).astype(BF)
+    held = add([held[0]] + [shift_x(held[s], s) for s in far_first(x_n)])
     return (held / (members_all - 1)).astype(BF)
 
 

time: 176 us -> 176 us (level)
  transfers between devices with their start and end apart: 27 -> 27, of which waited for: 14 -> 13; matrix products, arithmetic and copies ran while one was open for 11% -> 11% of each run, Pallas kernels for 17% -> 17%
where the time goes in v1:
time: 176 us; the launch traced here: 175 us
  waiting for transfers between devices  77.4 us (44%)
  starting transfers between devices  46.2 us (26%)
  Pallas kernels  30.3 us (17%)
  local copies, waits for them, and re-layouts  17 us (10%)
  other arithmetic  4 us (2%)
    ppermute x6, waiting for transfers between devices, shift_z(): lax.ppermute(a, 'col', [(seat(*p), seat(p[0] ^ s, p[1], p[2])) for p in s...  49 us
    pallas_call x3, Pallas kernels, on_device(): pl.pallas_call(functools.partial(member_kernel, var=var, slot_of_var=plac...  26.8 us
    ppermute x9, waiting for transfers between devices, shift_y(): return lax.ppermute(a, 'mem', [(i, i ^ s) for i in range(y_n)])  15.5 us
    ppermute x9, starting transfers between devices, shift_y(): return lax.ppermute(a, 'mem', [(i, i ^ s) for i in range(y_n)])  15 us
    reshape x1, local copies, waits for them, and re-layouts, on_device(): jnp.transpose(tiles, (0, 3, 1, 2)).reshape(columns, width, slots * width)  11.9 us
    all_to_all x1, waiting for transfers between devices, on_device(): arrived.append(lax.all_to_all(pieces[1], 'col', 0, 0))  9.03 us
    ppermute x6, starting transfers between devices, shift_x(): lax.ppermute(a, 'col', [(seat(*p), seat(p[0], p[1] ^ s, p[2])) for p in s...  8.5 us
    ppermute x6, starting transfers between devices, shift_z(): lax.ppermute(a, 'col', [(seat(*p), seat(p[0] ^ s, p[1], p[2])) for p in s...  8.35 us
  transfers between devices with their start and end apart: 27, of which 13 were waited for; matrix products, arithmetic and copies ran while one was open for 11% of the time, Pallas kernels for 17%

profile of v1, /device:TPU:0, one launch (start us, length us, event | category | flops | bytes accessed | tf_op | source)
XLA Modules:
  0.0 175.3 jit_solution(1725574553817927174)
XLA Ops:
  1.6 2.1 %collective-permute-start.2 = (bf16[3,32,128]{2,1,0:T(8,128)(2,1)}, bf16[3,32,128]{2,1,0:T(8,128)(2,1)S(1)}, u32[]{:S(2)}, u32[]{:S(2)}) collective-permute-start(bf16[3,32,128]{2,1,0:T(8,128)(2,1)} %param.7), channel_id=1, source_target_pairs={{0,6},{1,7},{2,4},{3,5},{4,2},{5,3},{6,0},{7,1},{8,14},{9,15},{10,... | collective-permute-start | bytes 73736 | tf_op jit(solution)/shard_map/ppermute | solution.py:177
  4.3 3.6 %cut.1 = bf16[32,2,2,128,128]{4,3,2,1,0:T(8,128)(2,1)} custom-call(bf16[32,2,3,128,128]{4,3,2,1,0:T(8,128)(2,1)} %bitcast.90), custom_call_target="tpu_custom_call" | custom-call | tf_op jit(solution)/shard_map/cut/pallas_call | solution.py:189
  9.3 6.9 %all-to-all-start = ((bf16[32,2,2,128,128]{4,3,2,1,0:T(8,128)(2,1)}), bf16[32,2,2,128,128]{4,3,2,1,0:T(8,128)(2,1)}, u32[]{:S(2)}, u32[]{:S(2)}) async-start(bf16[32,2,2,128,128]{4,3,2,1,0:T(8,128)(2,1)} %cut.1), calls=%async_computation | async-start | bytes 8388608 | tf_op jit(solution)/shard_map/all_to_all | solution.py:209
  16.2 3.1 %collective-permute-start.5 = (bf16[4,3,32,128]{3,2,1,0:T(8,128)(2,1)S(1)}, bf16[4,3,32,128]{3,2,1,0:T(8,128)(2,1)S(1)}, u32[]{:S(2)}, u32[]{:S(2)}) collective-permute-start(bf16[4,3,32,128]{3,2,1,0:T(8,128)(2,1)S(1)} %pad_maximum_fusion.4), channel_id=1, source_target_pairs={{0,24},{1,25},{2,26},{3,27},{4,28},{5,29},{6,30},{7,31},{8,16},{9,... | collective-permute-start | bytes 294920 | tf_op jit(solution)/shard_map/ppermute | solution.py:174
  20.4 3.2 %slice.72 = bf16[32,2,1,128,128]{4,3,2,1,0:T(8,128)(2,1)} slice(bf16[32,2,3,128,128]{4,3,2,1,0:T(8,128)(2,1)} %bitcast.91), slice={[0:32], [0:2], [2:3], [0:128], [0:128]} | slice | bytes 4194304 | tf_op jit(solution)/shard_map/slice | solution.py:188
  23.6 45.0 %collective-permute-done.5 = bf16[4,3,32,128]{3,2,1,0:T(8,128)(2,1)S(1)} collective-permute-done((bf16[4,3,32,128]{3,2,1,0:T(8,128)(2,1)S(1)}, bf16[4,3,32,128]{3,2,1,0:T(8,128)(2,1)S(1)}, u32[]{:S(2)}, u32[]{:S(2)}) %collective-permute-start.5) | collective-permute-done | bytes 98336 | tf_op jit(solution)/shard_map/ppermute | solution.py:174
  68.6 3.1 %collective-permute-start.8 = (bf16[4,4,3,32,128]{4,3,2,1,0:T(8,128)(2,1)S(1)}, bf16[4,4,3,32,128]{4,3,2,1,0:T(8,128)(2,1)S(1)}, u32[]{:S(2)}, u32[]{:S(2)}) collective-permute-start(bf16[4,4,3,32,128]{4,3,2,1,0:T(8,128)(2,1)S(1)} %pad_maximum_fusion.1), channel_id=1, source_target_pairs={{0,96},{32,64},{64,32},{96,0},{1,97},{33,65},{65,33},{97,1},{2,98}... | collective-permute-start | bytes 1179656 | tf_op jit(solution)/shard_map/ppermute | solution.py:171
  72.8 11.9 %copy.38.tiles_ref = bf16[32,128,1024]{2,1,0:T(8,128)(2,1)} copy(bf16[32,128,1024]{1,2,0:T(8,128)(2,1)} %bitcast.92) | data formatting | bytes 16777216 | tf_op jit(solution)/shard_map/reshape | solution.py:211
  84.8 4.3 %collective-permute-done.8 = bf16[4,4,3,32,128]{4,3,2,1,0:T(8,128)(2,1)S(1)} collective-permute-done((bf16[4,4,3,32,128]{4,3,2,1,0:T(8,128)(2,1)S(1)}, bf16[4,4,3,32,128]{4,3,2,1,0:T(8,128)(2,1)S(1)}, u32[]{:S(2)}, u32[]{:S(2)}) %collective-permute-start.8) | collective-permute-done | bytes 393248 | tf_op jit(solution)/shard_map/ppermute | solution.py:171
  90.1 6.7 %all-to-all-start.1 = ((bf16[32,2,1,128,128]{4,3,2,1,0:T(8,128)(2,1)}), bf16[32,2,1,128,128]{4,3,2,1,0:T(8,128)(2,1)}, u32[]{:S(2)}, u32[]{:S(2)}) async-start(bf16[32,2,1,128,128]{4,3,2,1,0:T(8,128)(2,1)} %slice.72), calls=%async_computation.1 | async-start | bytes 4194304 | tf_op jit(solution)/shard_map/all_to_all | solution.py:216
  97.3 9.2 %shard_map.65 = (bf16[4,4,4,32,128]{4,3,2,1,0:T(8,128)(2,1)S(1)}, bf16[4,4,4,32,128]{4,3,2,1,0:T(8,128)(2,1)}) custom-call(s32[4]{0:T(128)S(1)} %pad_add_fusion.where_ref, s32[32,8]{1,0:T(8,128)S(1)} %copy.23.cols_ref, bf16[32,2,2,128,128]{4,3,2,1,0:T(8,128)(2,1)} %all-to-all-done.ens_ref, bf16[4,4,4,3,32,128]{5,4,3,2,1,0:T(8,128)(2,1)S(1)} %pad_maximum_fusion.mine_ref, ...), custom_call_target="tpu_custom_call" | custom-call | tf_op jit(solution)/shard_map/pallas_call | solution.py:242
  107.5 9.2 %shard_map.64 = (bf16[4,4,4,32,128]{4,3,2,1,0:T(8,128)(2,1)S(1)}, bf16[4,4,4,32,128]{4,3,2,1,0:T(8,128)(2,1)}) custom-call(s32[4]{0:T(128)S(1)} %pad_add_fusion.where_ref, s32[32,8]{1,0:T(8,128)S(1)} %copy.23.cols_ref, bf16[32,2,2,128,128]{4,3,2,1,0:T(8,128)(2,1)} %all-to-all-done.ens_ref, bf16[4,4,4,3,32,128]{5,4,3,2,1,0:T(8,128)(2,1)S(1)} %pad_maximum_fusion.mine_ref, ...), custom_call_target="tpu_custom_call" | custom-call | tf_op jit(solution)/shard_map/pallas_call | solution.py:242
  117.8 9.0 %all-to-all-done.1.ens_ref = bf16[32,2,1,128,128]{4,3,2,1,0:T(8,128)(2,1)} async-done(((bf16[32,2,1,128,128]{4,3,2,1,0:T(8,128)(2,1)}), bf16[32,2,1,128,128]{4,3,2,1,0:T(8,128)(2,1)}, u32[]{:S(2)}, u32[]{:S(2)}) %all-to-all-start.1) | async-done | bytes 2097184 | tf_op jit(solution)/shard_map/all_to_all | solution.py:216
  126.8 8.4 %shard_map.66 = (bf16[4,4,4,32,128]{4,3,2,1,0:T(8,128)(2,1)S(1)}, bf16[4,4,4,32,128]{4,3,2,1,0:T(8,128)(2,1)S(1)}) custom-call(s32[4]{0:T(128)S(1)} %pad_add_fusion.where_ref, s32[32,8]{1,0:T(8,128)S(1)} %copy.23.cols_ref, bf16[32,2,1,128,128]{4,3,2,1,0:T(8,128)(2,1)} %all-to-all-done.1.ens_ref, ...), custom_call_target="tpu_custom_call" | custom-call | tf_op jit(solution)/shard_map/pallas_call | solution.py:242
  137.9 3.1 %collective-permute-start.12 = (bf16[4,4,2,32,128]{4,3,1,0,2:T(8,128)(2,1)S(1)}, bf16[4,4,2,32,128]{4,3,1,0,2:T(8,128)(2,1)S(1)}, u32[]{:S(2)}, u32[]{:S(2)}) collective-permute-start(bf16[4,4,2,32,128]{4,3,1,0,2:T(8,128)(2,1)S(1)} %get-tuple-element.35), channel_id=1, source_target_pairs={{0,64},{32,96},{64,0},{96,32},{1,65},{33,97},{65,1},{97,33},{2,66}... | collective-permute-start | bytes 786440 | tf_op jit(solution)/shard_map/ppermute | solution.py:171
  142.3 3.1 %collective-permute-start.16 = (bf16[4,4,1,32,128]{4,3,1,0,2:T(8,128)(2,1)S(1)}, bf16[4,4,1,32,128]{4,3,1,0,2:T(8,128)(2,1)S(1)}, u32[]{:S(2)}, u32[]{:S(2)}) collective-permute-start(bf16[4,4,1,32,128]{4,3,1,0,2:T(8,128)(2,1)S(1)} %get-tuple-element.38), channel_id=1, source_target_pairs={{0,64},{32,96},{64,0},{96,32},{1,65},{33,97},{65,1},{97,33},{2,66}... | collective-permute-start | bytes 393224 | tf_op jit(solution)/shard_map/ppermute | solution.py:171
  146.1 2.6 %collective-permute-done.12 = bf16[4,4,2,32,128]{4,3,1,0,2:T(8,128)(2,1)S(1)} collective-permute-done((bf16[4,4,2,32,128]{4,3,1,0,2:T(8,128)(2,1)S(1)}, bf16[4,4,2,32,128]{4,3,1,0,2:T(8,128)(2,1)S(1)}, u32[]{:S(2)}, u32[]{:S(2)}) %collective-permute-start.12) | collective-permute-done | bytes 262176 | tf_op jit(solution)/shard_map/ppermute | solution.py:171
  148.7 2.9 %collective-permute-start.17 = (bf16[4,4,1,32,128]{4,3,1,0,2:T(8,128)(2,1)S(1)}, bf16[4,4,1,32,128]{4,3,1,0,2:T(8,128)(2,1)S(1)}, u32[]{:S(2)}, u32[]{:S(2)}) collective-permute-start(bf16[4,4,1,32,128]{4,3,1,0,2:T(8,128)(2,1)S(1)} %get-tuple-element.40), channel_id=1, source_target_pairs={{0,96},{32,64},{64,32},{96,0},{1,97},{33,65},{65,33},{97,1},{2,98}... | collective-permute-start | bytes 393224 | tf_op jit(solution)/shard_map/ppermute | solution.py:171
  151.6 2.9 %collective-permute-done.14 = bf16[4,4,2,32,128]{4,3,1,0,2:T(8,128)(2,1)S(1)} collective-permute-done((bf16[4,4,2,32,128]{4,3,1,0,2:T(8,128)(2,1)S(1)}, bf16[4,4,2,32,128]{4,3,1,0,2:T(8,128)(2,1)S(1)}, u32[]{:S(2)}, u32[]{:S(2)}) %collective-permute-start.14) | collective-permute-done | bytes 262176 | tf_op jit(solution)/shard_map/ppermute | solution.py:171
  154.7 2.5 %collective-permute-done.16 = bf16[4,4,1,32,128]{4,3,1,0,2:T(8,128)(2,1)S(1)} collective-permute-done((bf16[4,4,1,32,128]{4,3,1,0,2:T(8,128)(2,1)S(1)}, bf16[4,4,1,32,128]{4,3,1,0,2:T(8,128)(2,1)S(1)}, u32[]{:S(2)}, u32[]{:S(2)}) %collective-permute-start.16) | collective-permute-done | bytes 131104 | tf_op jit(solution)/shard_map/ppermute | solution.py:171
  157.2 2.5 %collective-permute-done.18 = bf16[4,4,1,32,128]{4,3,1,0,2:T(8,128)(2,1)S(1)} collective-permute-done((bf16[4,4,1,32,128]{4,3,1,0,2:T(8,128)(2,1)S(1)}, bf16[4,4,1,32,128]{4,3,1,0,2:T(8,128)(2,1)S(1)}, u32[]{:S(2)}, u32[]{:S(2)}) %collective-permute-start.18) | collective-permute-done | bytes 131104 | tf_op jit(solution)/shard_map/ppermute | solution.py:171
  160.9 3.0 %collective-permute-start.20 = (bf16[4,3,32,128]{3,2,0,1:T(8,128)(2,1)S(1)}, bf16[4,3,32,128]{3,2,0,1:T(8,128)(2,1)S(1)}, u32[]{:S(2)}, u32[]{:S(2)}) collective-permute-start(bf16[4,3,32,128]{3,2,0,1:T(8,128)(2,1)S(1)} %get-tuple-element.43), channel_id=1, source_target_pairs={{0,24},{1,25},{2,26},{3,27},{4,28},{5,29},{6,30},{7,31},{8,16},{9,... | collective-permute-start | bytes 294920 | tf_op jit(solution)/shard_map/ppermute | solution.py:174
  163.9 2.9 %collective-permute-done.19 = bf16[4,3,32,128]{3,2,0,1:T(8,128)(2,1)S(1)} collective-permute-done((bf16[4,3,32,128]{3,2,0,1:T(8,128)(2,1)S(1)}, bf16[4,3,32,128]{3,2,0,1:T(8,128)(2,1)S(1)}, u32[]{:S(2)}, u32[]{:S(2)}) %collective-permute-start.19) | collective-permute-done | bytes 98336 | tf_op jit(solution)/shard_map/ppermute | solution.py:174
  169.6 2.5 %collective-permute-start.23 = (bf16[3,32,128]{2,1,0:T(8,128)(2,1)S(1)}, bf16[3,32,128]{2,1,0:T(8,128)(2,1)S(1)}, u32[]{:S(2)}, u32[]{:S(2)}) collective-permute-start(bf16[3,32,128]{2,1,0:T(8,128)(2,1)S(1)} %get-tuple-element.46), channel_id=1, source_target_pairs={{0,6},{1,7},{2,4},{3,5},{4,2},{5,3},{6,0},{7,1},{8,14},{9,15},{10,... | collective-permute-start | bytes 73736 | tf_op jit(solution)/shard_map/ppermute | solution.py:177
  (73 shorter events, 21.2 us)
Async XLA Ops:
  0.0 7.9 %collective-permute-start = (bf16[3,32,128]{2,1,0:T(8,128)(2,1)}, bf16[3,32,128]{2,1,0:T(8,128)(2,1)S(1)}, u32[]{:S(2)}, u32[]{:S(2)}) collective-permute-start(bf16[3,32,128]{2,1,0:T(8,128)(2,1)} %param.7), channel_id=1, source_target_pairs={{0,2},{1,3},{2,0},{3,1},{4,6},{5,7},{6,4},{7,5},{8,10},{9,11},{10,... | collective-permute-start | bytes 73736 | tf_op jit(solution)/shard_map/ppermute | solution.py:177
  1.6 6.3 %collective-permute-start.2 = (bf16[3,32,128]{2,1,0:T(8,128)(2,1)}, bf16[3,32,128]{2,1,0:T(8,128)(2,1)S(1)}, u32[]{:S(2)}, u32[]{:S(2)}) collective-permute-start(bf16[3,32,128]{2,1,0:T(8,128)(2,1)} %param.7), channel_id=1, source_target_pairs={{0,6},{1,7},{2,4},{3,5},{4,2},{5,3},{6,0},{7,1},{8,14},{9,15},{10,... | collective-permute-start | bytes 73736 | tf_op jit(solution)/shard_map/ppermute | solution.py:177
  3.7 5.5 %collective-permute-start.1 = (bf16[3,32,128]{2,1,0:T(8,128)(2,1)}, bf16[3,32,128]{2,1,0:T(8,128)(2,1)S(1)}, u32[]{:S(2)}, u32[]{:S(2)}) collective-permute-start(bf16[3,32,128]{2,1,0:T(8,128)(2,1)} %param.7), channel_id=1, source_target_pairs={{0,4},{1,5},{2,6},{3,7},{4,0},{5,1},{6,2},{7,3},{8,12},{9,13},{10,... | collective-permute-start | bytes 73736 | tf_op jit(solution)/shard_map/ppermute | solution.py:177
  9.3 80.8 %all-to-all-start = ((bf16[32,2,2,128,128]{4,3,2,1,0:T(8,128)(2,1)}), bf16[32,2,2,128,128]{4,3,2,1,0:T(8,128)(2,1)}, u32[]{:S(2)}, u32[]{:S(2)}) async-start(bf16[32,2,2,128,128]{4,3,2,1,0:T(8,128)(2,1)} %cut.1), calls=%async_computation | async-start | bytes 8388608 | tf_op jit(solution)/shard_map/all_to_all | solution.py:209
  16.2 52.4 %collective-permute-start.5 = (bf16[4,3,32,128]{3,2,1,0:T(8,128)(2,1)S(1)}, bf16[4,3,32,128]{3,2,1,0:T(8,128)(2,1)S(1)}, u32[]{:S(2)}, u32[]{:S(2)}) collective-permute-start(bf16[4,3,32,128]{3,2,1,0:T(8,128)(2,1)S(1)} %pad_maximum_fusion.4), channel_id=1, source_target_pairs={{0,24},{1,25},{2,26},{3,27},{4,28},{5,29},{6,30},{7,31},{8,16},{9,... | collective-permute-start | bytes 294920 | tf_op jit(solution)/shard_map/ppermute | solution.py:174
  19.2 49.4 %collective-permute-start.4 = (bf16[4,3,32,128]{3,2,1,0:T(8,128)(2,1)S(1)}, bf16[4,3,32,128]{3,2,1,0:T(8,128)(2,1)S(1)}, u32[]{:S(2)}, u32[]{:S(2)}) collective-permute-start(bf16[4,3,32,128]{3,2,1,0:T(8,128)(2,1)S(1)} %pad_maximum_fusion.4), channel_id=1, source_target_pairs={{0,16},{1,17},{2,18},{3,19},{4,20},{5,21},{6,22},{7,23},{8,24},{9,... | collective-permute-start | bytes 294920 | tf_op jit(solution)/shard_map/ppermute | solution.py:174
  20.0 48.5 %collective-permute-start.3 = (bf16[4,3,32,128]{3,2,1,0:T(8,128)(2,1)S(1)}, bf16[4,3,32,128]{3,2,1,0:T(8,128)(2,1)S(1)}, u32[]{:S(2)}, u32[]{:S(2)}) collective-permute-start(bf16[4,3,32,128]{3,2,1,0:T(8,128)(2,1)S(1)} %pad_maximum_fusion.4), channel_id=1, source_target_pairs={{0,8},{1,9},{2,10},{3,11},{4,12},{5,13},{6,14},{7,15},{8,0},{9,1},... | collective-permute-start | bytes 294920 | tf_op jit(solution)/shard_map/ppermute | solution.py:174
  68.6 20.4 %collective-permute-start.8 = (bf16[4,4,3,32,128]{4,3,2,1,0:T(8,128)(2,1)S(1)}, bf16[4,4,3,32,128]{4,3,2,1,0:T(8,128)(2,1)S(1)}, u32[]{:S(2)}, u32[]{:S(2)}) collective-permute-start(bf16[4,4,3,32,128]{4,3,2,1,0:T(8,128)(2,1)S(1)} %pad_maximum_fusion.1), channel_id=1, source_target_pairs={{0,96},{32,64},{64,32},{96,0},{1,97},{33,65},{65,33},{97,1},{2,98}... | collective-permute-start | bytes 1179656 | tf_op jit(solution)/shard_map/ppermute | solution.py:171
  71.7 17.3 %collective-permute-start.7 = (bf16[4,4,3,32,128]{4,3,2,1,0:T(8,128)(2,1)S(1)}, bf16[4,4,3,32,128]{4,3,2,1,0:T(8,128)(2,1)S(1)}, u32[]{:S(2)}, u32[]{:S(2)}) collective-permute-start(bf16[4,4,3,32,128]{4,3,2,1,0:T(8,128)(2,1)S(1)} %pad_maximum_fusion.1), channel_id=1, source_target_pairs={{0,64},{32,96},{64,0},{96,32},{1,65},{33,97},{65,1},{97,33},{2,66}... | collective-permute-start | bytes 1179656 | tf_op jit(solution)/shard_map/ppermute | solution.py:171
  72.4 17.4 %collective-permute-start.6 = (bf16[4,4,3,32,128]{4,3,2,1,0:T(8,128)(2,1)S(1)}, bf16[4,4,3,32,128]{4,3,2,1,0:T(8,128)(2,1)S(1)}, u32[]{:S(2)}, u32[]{:S(2)}) collective-permute-start(bf16[4,4,3,32,128]{4,3,2,1,0:T(8,128)(2,1)S(1)} %pad_maximum_fusion.1), channel_id=1, source_target_pairs={{0,32},{32,0},{64,96},{96,64},{1,33},{33,1},{65,97},{97,65},{2,34}... | collective-permute-start | bytes 1179656 | tf_op jit(solution)/shard_map/ppermute | solution.py:171
  90.0 7.3 %collective-permute-start.9 = (bf16[4,4,4,3,32,128]{5,4,3,2,1,0:T(8,128)(2,1)S(1)}, bf16[4,4,4,3,32,128]{5,4,3,2,1,0:T(8,128)(2,1)S(1)}, u32[]{:S(2)}, u32[]{:S(2)}) collective-permute-start(bf16[4,4,4,3,32,128]{5,4,3,2,1,0:T(8,128)(2,1)S(1)} %pad_maximum_fusion.mine_ref), channel_id=1, source_target_pairs={{0,1},{1,0},{2,3},{3,2},{4,5},{5,4},{6,7},{7,6},{8,9},{9,8},{10,11... | collective-permute-start | bytes 4718600 | tf_op jit(solution)/shard_map/ppermute | solution.py:180
  90.1 36.8 %all-to-all-start.1 = ((bf16[32,2,1,128,128]{4,3,2,1,0:T(8,128)(2,1)}), bf16[32,2,1,128,128]{4,3,2,1,0:T(8,128)(2,1)}, u32[]{:S(2)}, u32[]{:S(2)}) async-start(bf16[32,2,1,128,128]{4,3,2,1,0:T(8,128)(2,1)} %slice.72), calls=%async_computation.1 | async-start | bytes 4194304 | tf_op jit(solution)/shard_map/all_to_all | solution.py:216
  107.3 28.0 %collective-permute-start.11 = (bf16[4,4,4,32,128]{4,3,2,1,0:T(8,128)(2,1)}, bf16[4,4,4,32,128]{4,3,2,1,0:T(8,128)(2,1)}, u32[]{:S(2)}, u32[]{:S(2)}) collective-permute-start(bf16[4,4,4,32,128]{4,3,2,1,0:T(8,128)(2,1)} %get-tuple-element.31), channel_id=1, source_target_pairs={{0,1},{1,0},{2,3},{3,2},{4,5},{5,4},{6,7},{7,6},{8,9},{9,8},{10,11... | collective-permute-start | bytes 1572872 | tf_op jit(solution)/shard_map/ppermute | solution.py:180
  117.5 19.1 %collective-permute-start.10 = (bf16[4,4,4,32,128]{4,3,2,1,0:T(8,128)(2,1)}, bf16[4,4,4,32,128]{4,3,2,1,0:T(8,128)(2,1)}, u32[]{:S(2)}, u32[]{:S(2)}) collective-permute-start(bf16[4,4,4,32,128]{4,3,2,1,0:T(8,128)(2,1)} %get-tuple-element.29), channel_id=1, source_target_pairs={{0,1},{1,0},{2,3},{3,2},{4,5},{5,4},{6,7},{7,6},{8,9},{9,8},{10,11... | collective-permute-start | bytes 1572872 | tf_op jit(solution)/shard_map/ppermute | solution.py:180
  135.2 6.8 %collective-permute-start.15 = (bf16[4,4,4,32,128]{4,3,2,1,0:T(8,128)(2,1)S(1)}, bf16[4,4,4,32,128]{4,3,2,1,0:T(8,128)(2,1)S(1)}, u32[]{:S(2)}, u32[]{:S(2)}) collective-permute-start(bf16[4,4,4,32,128]{4,3,2,1,0:T(8,128)(2,1)S(1)} %get-tuple-element.34), channel_id=1, source_target_pairs={{0,1},{1,0},{2,3},{3,2},{4,5},{5,4},{6,7},{7,6},{8,9},{9,8},{10,11... | collective-permute-start | bytes 1572872 | tf_op jit(solution)/shard_map/ppermute | solution.py:180
  137.9 10.8 %collective-permute-start.12 = (bf16[4,4,2,32,128]{4,3,1,0,2:T(8,128)(2,1)S(1)}, bf16[4,4,2,32,128]{4,3,1,0,2:T(8,128)(2,1)S(1)}, u32[]{:S(2)}, u32[]{:S(2)}) collective-permute-start(bf16[4,4,2,32,128]{4,3,1,0,2:T(8,128)(2,1)S(1)} %get-tuple-element.35), channel_id=1, source_target_pairs={{0,64},{32,96},{64,0},{96,32},{1,65},{33,97},{65,1},{97,33},{2,66}... | collective-permute-start | bytes 786440 | tf_op jit(solution)/shard_map/ppermute | solution.py:171
  141.0 13.5 %collective-permute-start.14 = (bf16[4,4,2,32,128]{4,3,1,0,2:T(8,128)(2,1)S(1)}, bf16[4,4,2,32,128]{4,3,1,0,2:T(8,128)(2,1)S(1)}, u32[]{:S(2)}, u32[]{:S(2)}) collective-permute-start(bf16[4,4,2,32,128]{4,3,1,0,2:T(8,128)(2,1)S(1)} %get-tuple-element.36), channel_id=1, source_target_pairs={{0,32},{32,0},{64,96},{96,64},{1,33},{33,1},{65,97},{97,65},{2,34}... | collective-permute-start | bytes 786440 | tf_op jit(solution)/shard_map/ppermute | solution.py:171
  141.7 12.8 %collective-permute-start.13 = (bf16[4,4,2,32,128]{4,3,1,0,2:T(8,128)(2,1)S(1)}, bf16[4,4,2,32,128]{4,3,1,0,2:T(8,128)(2,1)S(1)}, u32[]{:S(2)}, u32[]{:S(2)}) collective-permute-start(bf16[4,4,2,32,128]{4,3,1,0,2:T(8,128)(2,1)S(1)} %get-tuple-element.37), channel_id=1, source_target_pairs={{0,96},{32,64},{64,32},{96,0},{1,97},{33,65},{65,33},{97,1},{2,98}... | collective-permute-start | bytes 786440 | tf_op jit(solution)/shard_map/ppermute | solution.py:171
  142.3 14.9 %collective-permute-start.16 = (bf16[4,4,1,32,128]{4,3,1,0,2:T(8,128)(2,1)S(1)}, bf16[4,4,1,32,128]{4,3,1,0,2:T(8,128)(2,1)S(1)}, u32[]{:S(2)}, u32[]{:S(2)}) collective-permute-start(bf16[4,4,1,32,128]{4,3,1,0,2:T(8,128)(2,1)S(1)} %get-tuple-element.38), channel_id=1, source_target_pairs={{0,64},{32,96},{64,0},{96,32},{1,65},{33,97},{65,1},{97,33},{2,66}... | collective-permute-start | bytes 393224 | tf_op jit(solution)/shard_map/ppermute | solution.py:171
  145.4 14.3 %collective-permute-start.18 = (bf16[4,4,1,32,128]{4,3,1,0,2:T(8,128)(2,1)S(1)}, bf16[4,4,1,32,128]{4,3,1,0,2:T(8,128)(2,1)S(1)}, u32[]{:S(2)}, u32[]{:S(2)}) collective-permute-start(bf16[4,4,1,32,128]{4,3,1,0,2:T(8,128)(2,1)S(1)} %get-tuple-element.39), channel_id=1, source_target_pairs={{0,32},{32,0},{64,96},{96,64},{1,33},{33,1},{65,97},{97,65},{2,34}... | collective-permute-start | bytes 393224 | tf_op jit(solution)/shard_map/ppermute | solution.py:171
  148.7 11.0 %collective-permute-start.17 = (bf16[4,4,1,32,128]{4,3,1,0,2:T(8,128)(2,1)S(1)}, bf16[4,4,1,32,128]{4,3,1,0,2:T(8,128)(2,1)S(1)}, u32[]{:S(2)}, u32[]{:S(2)}) collective-permute-start(bf16[4,4,1,32,128]{4,3,1,0,2:T(8,128)(2,1)S(1)} %get-tuple-element.40), channel_id=1, source_target_pairs={{0,96},{32,64},{64,32},{96,0},{1,97},{33,65},{65,33},{97,1},{2,98}... | collective-permute-start | bytes 393224 | tf_op jit(solution)/shard_map/ppermute | solution.py:171
  159.8 7.1 %collective-permute-start.19 = (bf16[4,3,32,128]{3,2,0,1:T(8,128)(2,1)S(1)}, bf16[4,3,32,128]{3,2,0,1:T(8,128)(2,1)S(1)}, u32[]{:S(2)}, u32[]{:S(2)}) collective-permute-start(bf16[4,3,32,128]{3,2,0,1:T(8,128)(2,1)S(1)} %get-tuple-element.41), channel_id=1, source_target_pairs={{0,16},{1,17},{2,18},{3,19},{4,20},{5,21},{6,22},{7,23},{8,24},{9,... | collective-permute-start | bytes 294920 | tf_op jit(solution)/shard_map/ppermute | solution.py:174
  160.9 5.9 %collective-permute-start.21 = (bf16[4,3,32,128]{3,2,0,1:T(8,128)(2,1)S(1)}, bf16[4,3,32,128]{3,2,0,1:T(8,128)(2,1)S(1)}, u32[]{:S(2)}, u32[]{:S(2)}) collective-permute-start(bf16[4,3,32,128]{3,2,0,1:T(8,128)(2,1)S(1)} %get-tuple-element.42), channel_id=1, source_target_pairs={{0,8},{1,9},{2,10},{3,11},{4,12},{5,13},{6,14},{7,15},{8,0},{9,1},... | collective-permute-start | bytes 294920 | tf_op jit(solution)/shard_map/ppermute | solution.py:174
  160.9 6.9 %collective-permute-start.20 = (bf16[4,3,32,128]{3,2,0,1:T(8,128)(2,1)S(1)}, bf16[4,3,32,128]{3,2,0,1:T(8,128)(2,1)S(1)}, u32[]{:S(2)}, u32[]{:S(2)}) collective-permute-start(bf16[4,3,32,128]{3,2,0,1:T(8,128)(2,1)S(1)} %get-tuple-element.43), channel_id=1, source_target_pairs={{0,24},{1,25},{2,26},{3,27},{4,28},{5,29},{6,30},{7,31},{8,16},{9,... | collective-permute-start | bytes 294920 | tf_op jit(solution)/shard_map/ppermute | solution.py:174
  (11 other events, 53.2 us)
